TPU v7x, 256 devices: a whole 4x4x8 slice. The times are simulated.
256 devices in a mesh: group: 8 (over x, core), expert: 8 (over z), hid: 4 (over y).
Axes of the slice: x: 4, y: 4, z: 8, core: 2. Of those that a mesh axis runs over, the one named last changes fastest.
Arguments:
- tokens: bfloat16 [2048, 4096], P(('group', 'expert', 'hid')), may hold values from -6 to 6
- expert_ids: int32 [2048, 2], P(('group', 'expert', 'hid')), may hold values from 0 to 7, all different within a row; in each aligned block of 8 rows (0 to 7, 8 to 15, ...) at most 4 rows name the same one
- gate_numer: int32 [2048, 2], P(('group', 'expert', 'hid')), may hold values from 8 to 64
- gate_weight: bfloat16 [8, 4096, 14336], P('group', None, ('expert', 'hid')), may hold values from -0.09375 to 0.09375
- up_weight: bfloat16 [8, 4096, 14336], P('group', None, ('expert', 'hid')), may hold values from -0.09375 to 0.09375
- down_weight: bfloat16 [8, 14336, 4096], P('group', ('expert', 'hid')), may hold values from -0.046875 to 0.046875
Outputs:
- mixed: bfloat16 [2048, 4096], P(('group', 'expert', 'hid'))
Inputs may be any that keep to these rules, and one draw needn't show every extreme that they name: `expert_ids`: A token's 2 ids differ. Within the rows of one device (aligned blocks of 8 rows) no expert is named more than 4 times, and in every draw some block names some expert exactly 4 times.
All inputs are finite; a program needn't handle non-finite values.
Results may differ from a plain program's by a relative error of at most 0.018.
Values may be sent and summed in bfloat16 or wider, within the bound.
No kernel may reach another device: no remote copies, remote signals or barrier semaphores. Data moves between devices by JAX's collectives and lax.ppermute only.
A program may use at most 128 MiB of HBM per device.

v0:
```python
import jax
import jax.numpy as jnp
from jax import lax
from jax.sharding import PartitionSpec as P

TOPK = 2
CAP = 4


def expert_block(block, w_gate, w_up, w_down):
    local = w_gate.shape[0]
    grid = block.reshape(-1, local, CAP, block.shape[-1])
    gate = jnp.einsum("mlcd,ldf->mlcf", grid, w_gate, preferred_element_type=jnp.float32)
    upper = jnp.einsum("mlcd,ldf->mlcf", grid, w_up, preferred_element_type=jnp.float32)
    hidden = (jax.nn.silu(gate) * upper).astype(jnp.bfloat16)
    output = jnp.einsum("mlcf,lfd->mlcd", hidden, w_down, preferred_element_type=jnp.float32)
    return output.reshape(block.shape)


def body(tokens, expert_ids, gate_numer, gate_weight, up_weight, down_weight):
    tok = tokens.shape[0]
    width = tokens.shape[1]
    groups = lax.axis_size("group")
    members = lax.axis_size(("expert", "hid"))
    local = gate_weight.shape[0]
    experts = groups * local
    flat = expert_ids.reshape(tok * TOPK)
    onehot = (flat[:, None] == jnp.arange(experts, dtype=jnp.int32)[None, :]).astype(jnp.int32)
    before = jnp.cumsum(onehot, axis=0) - onehot
    place = jnp.sum(before * onehot, axis=1)
    target = flat * CAP + place
    slot_ids = jnp.arange(experts * CAP, dtype=jnp.int32)
    scatter_mat = (slot_ids[:, None] == target[None, :]).astype(jnp.bfloat16)
    collect_mat = (target[:, None] == slot_ids[None, :]).astype(jnp.bfloat16)
    copies = jnp.repeat(tokens, TOPK, axis=0)
    outgoing = jnp.dot(scatter_mat, copies, preferred_element_type=jnp.float32).astype(jnp.bfloat16)
    outgoing = outgoing.reshape(groups, local * CAP, width)
    arrived = lax.all_to_all(outgoing, "group", split_axis=0, concat_axis=0, tiled=True)
    partial_value = expert_block(
        lax.all_gather(arrived, ("expert", "hid"), axis=0, tiled=True),
        gate_weight,
        up_weight,
        down_weight,
    )
    partial_value = partial_value.reshape(members, groups, local * CAP, width)
    summed = lax.psum_scatter(
        partial_value.astype(jnp.bfloat16), ("expert", "hid"), scatter_dimension=0, tiled=True
    )
    returned = lax.all_to_all(summed, "group", split_axis=1, concat_axis=1, tiled=True)
    results = returned.reshape(experts * CAP, width)
    values = jnp.dot(collect_mat, results, preferred_element_type=jnp.float32)
    route_w = gate_numer.astype(jnp.float32) * (1.0 / 64.0)
    weighted = values.reshape(tok, TOPK, width) * route_w[:, :, None]
    return jnp.sum(weighted, axis=1).astype(jnp.bfloat16)


def solution(mesh):
    return jax.shard_map(
        body,
        mesh=mesh,
        in_specs=(
            P(("group", "expert", "hid"), None),
            P(("group", "expert", "hid"), None),
            P(("group", "expert", "hid"), None),
            P("group", None, ("expert", "hid")),
            P("group", None, ("expert", "hid")),
            P("group", ("expert", "hid"), None),
        ),
        out_specs=P(("group", "expert", "hid"), None),
        check_vma=False,
    )
```

profile of v0, /device:TPU:1, one launch (start us, length us, event | category | flops | bytes accessed | tf_op | source)
XLA Modules:
  0.0 374.8 jit_solution(6712984873349726699)
XLA Ops:
  6.5 0.0 all-gather.2.cloned.1.call-start
  6.5 0.8 copy.27
  7.3 0.1 eq.57
  7.4 0.1 fusion.19
  7.5 0.2 select_reduce_fusion
  7.7 0.9 broadcast_in_dim.2
  8.6 0.1 reshape.74
  8.7 0.2 convolution_convert_fusion
  8.9 0.1 reshape.75
  9.0 12.1 %all_to_all.10 = bf16[8,4,4096]{2,1,0:T(4,128)(2,1)S(1)} all-to-all(bf16[8,4,4096]{2,1,0:T(4,128)(2,1)S(1)} %reshape.75), channel_id=1, replica_groups=mesh['group'=8,'expert'=8,'hid'=4] {'group'}, dimensions={0} | all-to-all | bytes 524288 | tf_op jit(solution)/shard_map/all_to_all | solution.py:38
  21.0 0.9 copy.30
  21.9 0.0 all-gather.2.cloned.1.call-update
  21.9 0.0 all-reduce.3.cloned.1.call-start
  22.0 98.7 %all-gather.2.cloned.1.call-done = bf16[256,4,4096]{2,0,1:T(8,128)(2,1)} async-done(((bf16[8,4,4096]{2,0,1:T(8,128)(2,1)}), bf16[256,4,4096]{2,0,1:T(8,128)(2,1)}) %all-gather.2.cloned.1.call-update) | async-done | bytes 8388624 | tf_op jit(solution)/shard_map/all_gather | solution.py:40
  120.7 7.5 %fusion.3 = f32[256,4,448]{0,2,1:T(8,128)S(1)} fusion(bf16[256,4,4096]{2,0,1:T(8,128)(2,1)} %all-gather.2.cloned.1.call-done, bf16[1,4096,448]{1,2,0:T(8,128)(2,1)} %param.9), kind=kOutput, calls=%fused_computation.6 | convolution fusion | flops 3758096384 | bytes 13893632 | tf_op jit(solution)/shard_map/mlcd,ldf->mlcf/dot_general | solution.py:13
  128.2 15.3 %convert_bitcast_fusion = bf16[32,8,4,4096]{3,1,0,2:T(8,128)(2,1)} fusion(bf16[1,448,4096]{2,1,0:T(8,128)(2,1)} %param.11, bf16[256,4,4096]{2,0,1:T(8,128)(2,1)} %all-gather.2.cloned.1.call-done, bf16[1,4096,448]{1,2,0:T(8,128)(2,1)} %param.10, f32[256,4,448]{0,2,1:T(8,128)S(1)} %fusion.3), kind=kOutput, calls=%fused_computation | convolution fusion | flops 7523139584 | bytes 25952256 | tf_op jit(solution)/shard_map/mlcf,lfd->mlcd/dot_general | solution.py:16
  143.4 0.0 copy-start.1
  143.4 0.0 copy-start
  143.5 0.0 all-reduce.3.cloned.1.call-update
  143.5 0.1 reduce_sum.21
  143.6 0.6 copy-done.1
  144.1 0.6 dynamic-slice
  144.7 208.3 %all-reduce.3.cloned.1.call-done = bf16[32,8,4,4096]{3,1,0,2:T(8,128)(2,1)} async-done(((bf16[32,8,4,4096]{3,1,0,2:T(8,128)(2,1)}), bf16[32,8,4,4096]{3,1,0,2:T(8,128)(2,1)}) %all-reduce.3.cloned.1.call-update) | async-done | bytes 8388624
  353.0 1.6 constant_dynamic-slice_fusion
  354.6 0.9 copy.31
  355.5 5.1 %all-to-all-start.1 = ((bf16[1,8,4,4096]{3,2,0,1:T(4,128)(2,1)}), bf16[1,8,4,4096]{3,2,0,1:T(4,128)(2,1)S(1)}, u32[]{:S(2)}, u32[]{:S(2)}) async-start(bf16[1,8,4,4096]{3,2,0,1:T(4,128)(2,1)} %copy.31), calls=%async_computation.1 | async-start | bytes 524288 | tf_op jit(solution)/shard_map/all_to_all | solution.py:49
  360.6 0.1 copy.29
  360.7 0.0 copy-done
  360.7 6.4 %all-to-all-done.1 = bf16[1,8,4,4096]{3,2,0,1:T(4,128)(2,1)S(1)} async-done(((bf16[1,8,4,4096]{3,2,0,1:T(4,128)(2,1)}), bf16[1,8,4,4096]{3,2,0,1:T(4,128)(2,1)S(1)}, u32[]{:S(2)}, u32[]{:S(2)}) %all-to-all-start.1) | async-done | bytes 262176 | tf_op jit(solution)/shard_map/all_to_all | solution.py:49
  367.1 0.1 reshape.84
  367.1 0.9 fusion.16
  (4 shorter events, 0.1 us)
Async XLA Ops:
  6.5 114.1 %all-gather.2.cloned.1.call-start = ((), (), s32[]{:S(2)}) async-start(), calls=%async_computation.2 | async-start | bytes 8650752 | tf_op jit(solution)/shard_map/all_gather | solution.py:40
  21.9 331.1 %all-reduce.3.cloned.1.call-start = ((), (), s32[]{:S(2)}) async-start(), calls=%async_computation.3 | async-start | bytes 16777216
  143.4 0.7 copy-start.1
  143.4 217.2 %copy-start = (s32[8,2]{0,1:T(2,128)S(1)}, s32[8,2]{0,1:T(2,128)}, u32[]{:S(2)}) copy-start(s32[8,2]{0,1:T(2,128)} %param.8) | copy-start | bytes 196
  355.5 11.6 %all-to-all-start.1 = ((bf16[1,8,4,4096]{3,2,0,1:T(4,128)(2,1)}), bf16[1,8,4,4096]{3,2,0,1:T(4,128)(2,1)S(1)}, u32[]{:S(2)}, u32[]{:S(2)}) async-start(bf16[1,8,4,4096]{3,2,0,1:T(4,128)(2,1)} %copy.31), calls=%async_computation.1 | async-start | bytes 524288 | tf_op jit(solution)/shard_map/all_to_all | solution.py:49
Sparse Core Ops, SparseCore 0:
  22.1 98.5 all-gather.1
  143.6 209.3 all-reduce.2
where the time goes:
time: 375 us
  waiting for transfers between devices  313 us (83%)
  matrix products  23.8 us (6%)
  between operations  13.5 us (4%)
  blocking collectives  12.1 us (3%)
  local copies, waits for them, and re-layouts  6.65 us (2%)
  starting transfers between devices  5.13 us (1%)
    unnamed x3, waiting for transfers between devices  208 us
    all_gather x1, waiting for transfers between devices, body(): lax.all_gather(arrived, ('expert', 'hid'), axis=0, tiled=True)  98.7 us
    dot_general x1, matrix products, expert_block(): jnp.einsum('mlcf,lfd->mlcd', hidden, w_down, preferred_element_type=jnp.f...  15.3 us
    all_to_all x1, blocking collectives, body(): lax.all_to_all(outgoing, 'group', split_axis=0, concat_axis=0, tiled=True)  12.1 us
    dot_general x1, matrix products, expert_block(): jnp.einsum('mlcd,ldf->mlcf', grid, w_gate, preferred_element_type=jnp.flo...  7.52 us
  transfers between devices with their start and end apart: 3, of which 3 were waited for; matrix products, arithmetic and copies ran while one was open for 0% of the time, Pallas kernels for 0%

commit v1 on v0

--- a/solution.py
+++ b/solution.py
@@ -37,7 +37,12 @@
     outgoing = outgoing.reshape(groups, local * CAP, width)
     arrived = lax.all_to_all(outgoing, "group", split_axis=0, concat_axis=0, tiled=True)
     partial_value = expert_block(
-        lax.all_gather(arrived, ("expert", "hid"), axis=0, tiled=True),
+        jnp.concatenate(
+            lax.all_to_all(
+                jnp.stack([arrived] * lax.axis_size(("expert", "hid"))), ("expert", "hid"), 0, 0
+            ),
+            axis=0,
+        ),
         gate_weight,
         up_weight,
         down_weight,

time: 375 us -> 471 us (1.26)
  blocking collectives: 12.1 us -> 207 us
  waiting for transfers between devices: 313 us -> 214 us
    all_to_all x0 -> x1, blocking collectives: none -> 195 us  [body(): lax.all_to_all(jnp.stack([arrived] * lax.axis_size(('expert', 'hid'))), (...]
    all_gather x1 -> x0, waiting for transfers between devices: 98.7 us -> none  [body(): lax.all_gather(arrived, ('expert', 'hid'), axis=0, tiled=True)]
    unnamed x3 -> x2, waiting for transfers between devices: 208 us -> 208 us
  transfers between devices with their start and end apart: 3 -> 2, of which waited for: 3 -> 2; matrix products, arithmetic and copies ran while one was open for 0% -> 0% of each run, Pallas kernels for 0% -> 0%
where the time goes in v1:
time: 471 us
  waiting for transfers between devices  214 us (45%)
  blocking collectives  207 us (44%)
  matrix products  20.5 us (4%)
  between operations  13.5 us (3%)
  local copies, waits for them, and re-layouts  10.2 us (2%)
  starting transfers between devices  5.09 us (1%)
    unnamed x2, waiting for transfers between devices  208 us
    all_to_all x1, blocking collectives, body(): lax.all_to_all(jnp.stack([arrived] * lax.axis_size(('expert', 'hid'))), (...  195 us
    dot_general x1, matrix products, expert_block(): jnp.einsum('mlcf,lfd->mlcd', hidden, w_down, preferred_element_type=jnp.f...  15.3 us
    all_to_all x1, blocking collectives, body(): lax.all_to_all(outgoing, 'group', split_axis=0, concat_axis=0, tiled=True)  12.1 us
  transfers between devices with their start and end apart: 2, of which 2 were waited for; matrix products, arithmetic and copies ran while one was open for 0% of the time, Pallas kernels for 0%

profile of v1, /device:TPU:1, one launch (start us, length us, event | category | flops | bytes accessed | tf_op | source)
XLA Modules:
  0.0 470.6 jit_solution(11304576026851386275)
XLA Ops:
  6.5 0.0 all-reduce.3.cloned.1.call-start
  6.5 0.8 copy.29
  7.3 0.1 eq.57
  7.4 0.1 fusion.29
  7.5 0.2 select_reduce_fusion
  7.7 0.9 broadcast_in_dim.2
  8.6 0.1 reshape.77
  8.7 0.2 convolution_convert_fusion
  8.9 0.1 reshape.78
  9.0 12.1 %all_to_all.15 = bf16[8,4,4096]{2,1,0:T(4,128)(2,1)S(1)} all-to-all(bf16[8,4,4096]{2,1,0:T(4,128)(2,1)S(1)} %reshape.78), channel_id=1, replica_groups=mesh['group'=8,'expert'=8,'hid'=4] {'group'}, dimensions={0} | all-to-all | bytes 524288 | tf_op jit(solution)/shard_map/all_to_all | solution.py:38
  21.0 0.1 copy.32
  21.2 1.0 stack.2
  22.2 0.0 copy-start.2
  22.3 194.5 %all_to_all.16 = bf16[32,8,4,4096]{3,1,2,0:T(8,128)(2,1)S(1)} all-to-all(bf16[32,8,4,4096]{3,1,2,0:T(8,128)(2,1)S(1)} %stack.2), channel_id=1, replica_groups=mesh['group'=8,'expert'=8,'hid'=4] {'expert','hid'}, dimensions={0} | all-to-all | bytes 16777216 | tf_op jit(solution)/shard_map/all_to_all | solution.py:41
  216.8 0.0 copy-start
  216.8 3.2 copy-done
  220.0 0.0 copy-done.2
  220.0 4.1 fusion.2
  224.1 15.3 %convert_bitcast_fusion = bf16[32,8,4,4096]{3,1,0,2:T(8,128)(2,1)} fusion(bf16[1,448,4096]{2,1,0:T(8,128)(2,1)} %param.11, bf16[1,4096,448]{1,2,0:T(8,128)(2,1)} %param.10, bf16[32,8,4,4096]{3,1,2,0:T(8,128)(2,1)} %copy-done, f32[256,4,448]{0,2,1:T(8,128)S(1)} %fusion.2), kind=kOutput, calls=%fused_computation.4 | convolution fusion | flops 7523139584 | bytes 25952256 | tf_op jit(solution)/shard_map/mlcf,lfd->mlcd/dot_general | solution.py:16
  239.4 0.0 all-reduce.3.cloned.1.call-update
  239.4 0.1 reduce_sum.21
  239.5 0.6 copy-done.3
  240.1 0.6 dynamic-slice
  240.7 208.1 %all-reduce.3.cloned.1.call-done = bf16[32,8,4,4096]{3,1,0,2:T(8,128)(2,1)} async-done(((bf16[32,8,4,4096]{3,1,0,2:T(8,128)(2,1)}), bf16[32,8,4,4096]{3,1,0,2:T(8,128)(2,1)}) %all-reduce.3.cloned.1.call-update) | async-done | bytes 8388624
  448.7 1.6 constant_dynamic-slice_fusion
  450.3 0.9 copy.34
  451.2 5.1 %all-to-all-start.2 = ((bf16[1,8,4,4096]{3,2,0,1:T(4,128)(2,1)}), bf16[1,8,4,4096]{3,2,0,1:T(4,128)(2,1)S(1)}, u32[]{:S(2)}, u32[]{:S(2)}) async-start(bf16[1,8,4,4096]{3,2,0,1:T(4,128)(2,1)} %copy.34), calls=%async_computation.2 | async-start | bytes 524288 | tf_op jit(solution)/shard_map/all_to_all | solution.py:54
  456.3 0.1 copy.31
  456.4 0.0 copy-done.1
  456.4 6.4 %all-to-all-done.2 = bf16[1,8,4,4096]{3,2,0,1:T(4,128)(2,1)S(1)} async-done(((bf16[1,8,4,4096]{3,2,0,1:T(4,128)(2,1)}), bf16[1,8,4,4096]{3,2,0,1:T(4,128)(2,1)S(1)}, u32[]{:S(2)}, u32[]{:S(2)}) %all-to-all-start.2) | async-done | bytes 262176 | tf_op jit(solution)/shard_map/all_to_all | solution.py:54
  462.8 0.1 reshape.88
  462.9 0.9 fusion.26
  (6 shorter events, 0.1 us)
Async XLA Ops:
  6.5 442.2 %all-reduce.3.cloned.1.call-start = ((), (), s32[]{:S(2)}) async-start(), calls=%async_computation.3 | async-start | bytes 16777216
  22.2 197.7 %copy-start.2 = (bf16[1,4096,448]{1,2,0:T(8,128)(2,1)S(1)}, bf16[1,4096,448]{1,2,0:T(8,128)(2,1)}, u32[]{:S(2)}) copy-start(bf16[1,4096,448]{1,2,0:T(8,128)(2,1)} %param.9) | copy-start | bytes 11010052
  216.8 3.2 copy-start
  239.4 0.7 copy-start.3
  239.4 217.0 %copy-start.1 = (s32[8,2]{0,1:T(2,128)S(1)}, s32[8,2]{0,1:T(2,128)}, u32[]{:S(2)}) copy-start(s32[8,2]{0,1:T(2,128)} %param.8) | copy-start | bytes 196
  451.2 11.6 %all-to-all-start.2 = ((bf16[1,8,4,4096]{3,2,0,1:T(4,128)(2,1)}), bf16[1,8,4,4096]{3,2,0,1:T(4,128)(2,1)S(1)}, u32[]{:S(2)}, u32[]{:S(2)}) async-start(bf16[1,8,4,4096]{3,2,0,1:T(4,128)(2,1)} %copy.34), calls=%async_computation.2 | async-start | bytes 524288 | tf_op jit(solution)/shard_map/all_to_all | solution.py:54
Sparse Core Ops, SparseCore 0:
  239.5 209.1 all-reduce.2
